TPU v7x, 32 devices: a whole 2x2x4 slice. The times are simulated.
32 devices in a mesh: gy: 4 (over x, core), gx: 8 (over z, y).
Axes of the slice: x: 2, y: 2, z: 4, core: 2. Of those that a mesh axis runs over, the one named last changes fastest.
Arguments:
- tokens: bfloat16 [32, 128, 384], P('gy', 'gx'), may hold values from -6 to 6
- w_qkv: bfloat16 [384, 1152], replicated, may hold values from -1 to 1
- w_out: bfloat16 [384, 384], replicated, may hold values from -0.3125 to 0.3125
- block_mask: int32 [4, 16], P('gy', 'gx'), may hold values from 0 to 1, as said below
- grad_out: bfloat16 [32, 128, 384], P('gy', 'gx'), may hold values from -6 to 6
Outputs:
- mixed: bfloat16 [32, 128, 384], P('gy', 'gx')
- d_tokens: bfloat16 [32, 128, 384], P('gy', 'gx')
Inputs may be any that keep to these rules, and one draw needn't show every extreme that they name: `block_mask`: 1 marks a tissue block, 0 background.
All inputs are finite; a program needn't handle non-finite values.
Results may differ from a plain program's by a relative error of at most 0.017.
Values may be sent and summed in bfloat16 or wider, within the bound.
No kernel may reach another device: no remote copies, remote signals or barrier semaphores. Data moves between devices by JAX's collectives and lax.ppermute only.
A program may use at most 64 MiB of HBM per device.

v0:
```python
import jax
import jax.numpy as jnp
from jax import lax
from jax.sharding import PartitionSpec as P

NH = 6
HEAD_SIZE = 64
KS = 7
TISSUE_BLOCK = 8
NEG_FILL = -1e30


def with_halo(x, sides, width):
    for axis, dim in sides:
        size, length = (lax.axis_size(axis), x.shape[dim])
        up = [(i, (i + 1) % size) for i in range(size - 1)]
        down = [(j, i) for i, j in up]
        last = lax.slice_in_dim(x, length - width, length, axis=dim)
        first = lax.slice_in_dim(x, 0, width, axis=dim)
        before = lax.ppermute(last, axis, up)
        after = lax.ppermute(first, axis, down)
        x = jnp.concatenate([before, x, after], axis=dim)
    return x


def from_behind(value, axis, steps):
    count = lax.axis_size(axis)
    first, last = (max(0, -steps), min(count, count - steps))
    return lax.ppermute(value, axis, [(source, source + steps) for source in range(first, last)])


def block_means(field):
    tile_rows, tile_cols, width = field.shape
    grouped = field.astype(jnp.float32).reshape(
        tile_rows // TISSUE_BLOCK, TISSUE_BLOCK, tile_cols // TISSUE_BLOCK, TISSUE_BLOCK, width
    )
    return (jnp.sum(grouped, axis=(1, 3)) / TISSUE_BLOCK).reshape(-1, width)


def spread_blocks(blocks, tile_rows, tile_cols):
    shaped = blocks.reshape(tile_rows // TISSUE_BLOCK, tile_cols // TISSUE_BLOCK, -1)
    return jnp.repeat(jnp.repeat(shaped, TISSUE_BLOCK, 0), TISSUE_BLOCK, 1).reshape(
        tile_rows * tile_cols, -1
    )


def moving_window(extended, row_start, col_start, tile_rows, tile_cols):
    starts = (row_start, col_start) + tuple((0 for _ in extended.shape[2:]))
    extent = (tile_rows, tile_cols) + tuple(extended.shape[2:])
    return lax.dynamic_slice(extended, starts, extent)


def local(tokens, w_qkv, w_out, block_mask, grad_out):
    tile_rows, tile_cols, width = tokens.shape
    reachable_cells = KS // 2
    position_total = KS * KS
    token_count = tile_rows * tile_cols
    score_scale = HEAD_SIZE ** (-0.5)
    flat_tokens = tokens.reshape(token_count, width)
    qkv = jnp.dot(flat_tokens, w_qkv, preferred_element_type=jnp.float32).astype(jnp.bfloat16)
    query = qkv[:, :width].reshape(tile_rows, tile_cols, width)
    keys = qkv[:, width : 2 * width].reshape(tile_rows, tile_cols, width)
    values = qkv[:, 2 * width :].reshape(tile_rows, tile_cols, width)
    token_flag = spread_blocks(block_mask.astype(jnp.float32), tile_rows, tile_cols)
    row_place = (
        lax.axis_index("gy") * tile_rows
        + jnp.arange(tile_rows + 2 * reachable_cells)
        - reachable_cells
    )
    col_place = (
        lax.axis_index("gx") * tile_cols
        + jnp.arange(tile_cols + 2 * reachable_cells)
        - reachable_cells
    )
    row_inside = (row_place >= 0) & (row_place < tile_rows * lax.axis_size("gy"))
    col_inside = (col_place >= 0) & (col_place < tile_cols * lax.axis_size("gx"))
    inside = row_inside[:, None] & col_inside[None, :]

    def window(extended, position):
        return moving_window(extended, position // KS, position % KS, tile_rows, tile_cols)

    pooled_keys = block_means(keys).astype(jnp.bfloat16)
    pooled_vals = block_means(values).astype(jnp.bfloat16)
    pool_flag = block_mask.reshape(-1).astype(jnp.bfloat16)
    kv_ext = with_halo(
        jnp.concatenate([keys, values], axis=2), (("gy", 0), ("gx", 1)), reachable_cells
    )
    row_keys, row_vals, row_flag = (
        lax.all_gather(pooled_keys, "gx", axis=0, tiled=True),
        lax.all_gather(pooled_vals, "gx", axis=0, tiled=True),
        lax.all_gather(pool_flag, "gx", axis=0, tiled=True),
    )
    col_keys, col_vals, col_flag = (
        lax.all_gather(pooled_keys, "gy", axis=0, tiled=True),
        lax.all_gather(pooled_vals, "gy", axis=0, tiled=True),
        lax.all_gather(pool_flag, "gy", axis=0, tiled=True),
    )
    query_heads = query.reshape(token_count, NH, HEAD_SIZE)

    def score_step(position, collected):
        key_win = window(kv_ext, position)[:, :, :width].reshape(token_count, NH, HEAD_SIZE)
        scores = (
            jnp.einsum("tnd,tnd->nt", query_heads, key_win, preferred_element_type=jnp.float32)
            * score_scale
        )
        valid = window(inside, position).reshape(token_count)
        masked = jnp.where(valid[None, :], scores, NEG_FILL)
        return lax.dynamic_update_index_in_dim(collected, masked, position, 0)

    local_s = lax.fori_loop(
        0, position_total, score_step, jnp.zeros((position_total, NH, token_count), jnp.float32)
    )

    def pool_scores(pool_keys, flags):
        scores = (
            jnp.einsum(
                "tnd,pnd->ntp",
                query_heads,
                pool_keys.reshape(-1, NH, HEAD_SIZE),
                preferred_element_type=jnp.float32,
            )
            * score_scale
        )
        return jnp.where(flags[None, None, :] > 0, scores, NEG_FILL)

    row_s = pool_scores(row_keys, row_flag)
    col_s = pool_scores(col_keys, col_flag)
    top = jnp.maximum(jnp.maximum(jnp.max(local_s, 0), jnp.max(row_s, -1)), jnp.max(col_s, -1))
    total = (
        jnp.sum(jnp.exp(local_s - top), 0)
        + jnp.sum(jnp.exp(row_s - top[:, :, None]), -1)
        + jnp.sum(jnp.exp(col_s - top[:, :, None]), -1)
    )
    lse = top + jnp.log(total)
    local_probs = jnp.exp(local_s - lse)
    row_pf = jnp.exp(row_s - lse[:, :, None])
    col_pf = jnp.exp(col_s - lse[:, :, None])
    row_ph = row_pf.astype(jnp.bfloat16)
    col_ph = col_pf.astype(jnp.bfloat16)

    def value_step(position, output):
        value_win = window(kv_ext, position)[:, :, width:].reshape(token_count, NH, HEAD_SIZE)
        probs = lax.dynamic_index_in_dim(local_probs, position, 0, keepdims=False)
        return output + probs.T[:, :, None] * value_win

    output = lax.fori_loop(
        0, position_total, value_step, jnp.zeros((token_count, NH, HEAD_SIZE), jnp.float32)
    )
    output = output + jnp.einsum(
        "ntp,pnd->tnd",
        row_ph,
        row_vals.reshape(-1, NH, HEAD_SIZE),
        preferred_element_type=jnp.float32,
    )
    output = output + jnp.einsum(
        "ntp,pnd->tnd",
        col_ph,
        col_vals.reshape(-1, NH, HEAD_SIZE),
        preferred_element_type=jnp.float32,
    )
    attended = output.reshape(token_count, width).astype(jnp.bfloat16)
    gated = attended * token_flag.astype(jnp.bfloat16)
    mixed = (
        flat_tokens.astype(jnp.float32) + jnp.dot(gated, w_out, preferred_element_type=jnp.float32)
    ).astype(jnp.bfloat16)
    grad_flat = grad_out.reshape(token_count, width)
    d_att = (
        jnp.einsum("tc,ec->te", grad_flat, w_out, preferred_element_type=jnp.float32) * token_flag
    ).astype(jnp.bfloat16)
    datt_heads = d_att.reshape(token_count, NH, HEAD_SIZE)
    delta = jnp.einsum(
        "tnd,tnd->nt",
        datt_heads,
        attended.reshape(token_count, NH, HEAD_SIZE),
        preferred_element_type=jnp.float32,
    )

    def pool_backward(prob_full, prob_half, pool_keys, pool_vals):
        key_heads = pool_keys.reshape(-1, NH, HEAD_SIZE)
        value_heads = pool_vals.reshape(-1, NH, HEAD_SIZE)
        prob_grad = jnp.einsum(
            "tnd,pnd->ntp", datt_heads, value_heads, preferred_element_type=jnp.float32
        )
        score_grad = (prob_full * (prob_grad - delta[:, :, None])).astype(jnp.bfloat16)
        query_part = (
            jnp.einsum("ntp,pnd->tnd", score_grad, key_heads, preferred_element_type=jnp.float32)
            * score_scale
        )
        key_part = (
            jnp.einsum("ntp,tnd->pnd", score_grad, query_heads, preferred_element_type=jnp.float32)
            * score_scale
        )
        value_part = jnp.einsum(
            "ntp,tnd->pnd", prob_half, datt_heads, preferred_element_type=jnp.float32
        )
        return (query_part, key_part.reshape(-1, width), value_part.reshape(-1, width))

    row_dq, row_dk, row_dv = pool_backward(row_pf, row_ph, row_keys, row_vals)
    col_dq, col_dk, col_dv = pool_backward(col_pf, col_ph, col_keys, col_vals)
    block_count = pooled_keys.shape[0]
    whole_row_dk, whole_row_dv = (
        lax.psum(row_dk.astype(jnp.bfloat16), "gx").astype(jnp.float32),
        lax.psum(row_dv.astype(jnp.bfloat16), "gx").astype(jnp.float32),
    )
    whole_col_dk, whole_col_dv = (
        lax.psum(col_dk.astype(jnp.bfloat16), "gy").astype(jnp.float32),
        lax.psum(col_dv.astype(jnp.bfloat16), "gy").astype(jnp.float32),
    )
    row_start = lax.axis_index("gx") * block_count
    col_start = lax.axis_index("gy") * block_count
    own_row_dk = lax.dynamic_slice_in_dim(whole_row_dk, row_start, block_count, 0)
    own_row_dv = lax.dynamic_slice_in_dim(whole_row_dv, row_start, block_count, 0)
    own_col_dk = lax.dynamic_slice_in_dim(whole_col_dk, col_start, block_count, 0)
    own_col_dv = lax.dynamic_slice_in_dim(whole_col_dv, col_start, block_count, 0)

    def query_step(position, grad_query):
        both_win = window(kv_ext, position)
        key_win = both_win[:, :, :width].reshape(token_count, NH, HEAD_SIZE)
        value_win = both_win[:, :, width:].reshape(token_count, NH, HEAD_SIZE)
        prob_grad = jnp.einsum(
            "tnd,tnd->nt", datt_heads, value_win, preferred_element_type=jnp.float32
        )
        probs = lax.dynamic_index_in_dim(local_probs, position, 0, keepdims=False)
        score_grad = probs * (prob_grad - delta)
        return grad_query + (score_grad.T[:, :, None] * key_win * score_scale).reshape(
            token_count, width
        )

    grad_query = lax.fori_loop(
        0, position_total, query_step, (row_dq + col_dq).reshape(token_count, width)
    )

    def return_step(position, ext_grad):
        both_win = window(kv_ext, position)
        value_win = both_win[:, :, width:].reshape(token_count, NH, HEAD_SIZE)
        prob_grad = jnp.einsum(
            "tnd,tnd->nt", datt_heads, value_win, preferred_element_type=jnp.float32
        )
        probs = lax.dynamic_index_in_dim(local_probs, position, 0, keepdims=False)
        score_grad = probs * (prob_grad - delta)
        key_term = (score_grad.T[:, :, None] * query_heads * score_scale).reshape(
            tile_rows, tile_cols, width
        )
        value_term = (probs.T[:, :, None] * datt_heads).reshape(tile_rows, tile_cols, width)
        updated = window(ext_grad, position) + jnp.concatenate([key_term, value_term], axis=2)
        return lax.dynamic_update_slice(ext_grad, updated, (position // KS, position % KS, 0))

    ext_grad = lax.fori_loop(
        0,
        position_total,
        return_step,
        jnp.zeros(
            (tile_rows + 2 * reachable_cells, tile_cols + 2 * reachable_cells, 2 * width),
            jnp.float32,
        ),
    )
    col_moves = (
        (-1, slice(0, reachable_cells), slice(tile_cols, tile_cols + reachable_cells)),
        (
            1,
            slice(tile_cols + reachable_cells, tile_cols + 2 * reachable_cells),
            slice(reachable_cells, 2 * reachable_cells),
        ),
    )
    for step_by, source_span, target_span in col_moves:
        arrived = from_behind(ext_grad[:, source_span].astype(jnp.bfloat16), "gx", step_by).astype(
            jnp.float32
        )
        ext_grad = ext_grad.at[:, target_span].add(arrived)
    ext_grad = ext_grad[:, reachable_cells : reachable_cells + tile_cols]
    row_moves = (
        (-1, slice(0, reachable_cells), slice(tile_rows, tile_rows + reachable_cells)),
        (
            1,
            slice(tile_rows + reachable_cells, tile_rows + 2 * reachable_cells),
            slice(reachable_cells, 2 * reachable_cells),
        ),
    )
    for step_by, source_span, target_span in row_moves:
        arrived = from_behind(ext_grad[source_span].astype(jnp.bfloat16), "gy", step_by).astype(
            jnp.float32
        )
        ext_grad = ext_grad.at[target_span].add(arrived)
    own_grad = ext_grad[reachable_cells : reachable_cells + tile_rows].reshape(
        token_count, 2 * width
    )
    grad_keys = own_grad[:, :width]
    grad_vals = own_grad[:, width:]
    grad_keys = grad_keys + spread_blocks(
        (own_row_dk + own_col_dk) / TISSUE_BLOCK, tile_rows, tile_cols
    )
    grad_vals = grad_vals + spread_blocks(
        (own_row_dv + own_col_dv) / TISSUE_BLOCK, tile_rows, tile_cols
    )
    d_qkv = jnp.concatenate([grad_query, grad_keys, grad_vals], axis=1).astype(jnp.bfloat16)
    d_tokens = (
        grad_flat.astype(jnp.float32)
        + jnp.einsum("tf,cf->tc", d_qkv, w_qkv, preferred_element_type=jnp.float32)
    ).astype(jnp.bfloat16)
    return (
        mixed.reshape(tile_rows, tile_cols, width),
        d_tokens.reshape(tile_rows, tile_cols, width),
    )


def solution(mesh):
    placed = (P("gy", "gx", None), P(), P(), P("gy", "gx"), P("gy", "gx", None))
    return jax.shard_map(
        local,
        mesh=mesh,
        in_specs=placed,
        out_specs=(P("gy", "gx", None), P("gy", "gx", None)),
        check_vma=False,
    )
```

profile of v0, /device:TPU:1, one launch (start us, length us, event | category | flops | bytes accessed | tf_op | source)
XLA Modules:
  0.0 717.1 jit_solution(2901687024737776675)
XLA Ops:
  3.1 4.5 collective-permute-start
  9.6 21.7 %all-gather.2 = bf16[8,2,384]{2,1,0:T(2,128)(2,1)S(1)} all-gather(bf16[1,2,384]{2,1,0:T(2,128)(2,1)S(1)} %fusion.49), channel_id=1, replica_groups=mesh['gy'=4,'gx'=8] {'gx'}, dimensions={0}, use_global_device_ids=true | all-gather | bytes 13824 | tf_op jit(solution)/shard_map/all_gather | solution.py:89
  31.3 9.7 %all-gather.3 = bf16[4,2,384]{2,1,0:T(2,128)(2,1)S(1)} all-gather(bf16[1,2,384]{2,1,0:T(2,128)(2,1)S(1)} %fusion.49), channel_id=1, replica_groups=mesh['gy'=4,'gx'=8] {'gy'}, dimensions={0}, use_global_device_ids=true | all-gather | bytes 7680 | tf_op jit(solution)/shard_map/all_gather | solution.py:94
  44.1 16.2 %all-reduce = bf16[16]{0:T(256)(128)(2,1)S(1)} all-reduce(bf16[16]{0:T(256)(128)(2,1)S(1)} %dynamic-update-slice.12), channel_id=2, replica_groups=mesh['gy'=4,'gx'=8] {'gx'}, use_global_device_ids=true, to_apply=%add | all-reduce | flops 16 | bytes 64
  62.5 9.3 %all-reduce.1 = bf16[8]{0:T(256)(128)(2,1)S(1)} all-reduce(bf16[8]{0:T(256)(128)(2,1)S(1)} %dynamic-update-slice.13), channel_id=3, replica_groups=mesh['gy'=4,'gx'=8] {'gy'}, use_global_device_ids=true, to_apply=%add.1 | all-reduce | flops 8 | bytes 32
  77.0 21.3 %all-gather.4 = bf16[8,2,384]{2,1,0:T(2,128)(2,1)S(1)} all-gather(bf16[1,2,384]{2,1,0:T(2,128)(2,1)S(1)} %fusion.50), channel_id=1, replica_groups=mesh['gy'=4,'gx'=8] {'gx'}, dimensions={0}, use_global_device_ids=true | all-gather | bytes 13824 | tf_op jit(solution)/shard_map/all_gather | solution.py:90
  98.4 9.9 %all-gather.5 = bf16[4,2,384]{2,1,0:T(2,128)(2,1)S(1)} all-gather(bf16[1,2,384]{2,1,0:T(2,128)(2,1)S(1)} %fusion.50), channel_id=1, replica_groups=mesh['gy'=4,'gx'=8] {'gy'}, dimensions={0}, use_global_device_ids=true | all-gather | bytes 7680 | tf_op jit(solution)/shard_map/all_gather | solution.py:95
  110.5 37.0 %while.65 = (s32[]{:T(128)}, f32[49,6,128]{2,1,0:T(8,128)S(1)}, pred[14,22]{1,0:T(8,128)(4,1)S(1)}, bf16[14,22,768]{2,1,0:T(8,128)(2,1)S(1)}, bf16[128,6,64]{2,1...) while((s32[]{:T(128)}, f32[49,6,128]{2,1,0:T(8,128)S(1)}, ...), condition=%wide.region_1.0_spmd, body=%wide.region_0.0_spmd.sunk | while | flops 197396 | bytes 608564 | solution.py:110
  150.2 4.1 exp.21
  154.3 68.9 %while.68 = (s32[]{:T(128)}, f32[128,6,64]{2,1,0:T(8,128)S(1)}, f32[49,6,128]{1,2,0:T(8,128)}, bf16[14,22,768]{2,1,0:T(8,128)(2,1)S(1)}, s32[]{:T(128)}, /*index...) while((s32[]{:T(128)}, f32[128,6,64]{2,1,0:T(8,128)S(1)}, ...), condition=%wide.region_10.11_spmd.clone, body=%wide.region_9.10_spmd.clone.sunk | while | flops 196630 | bytes 1287498 | solution.py:146
  228.7 43.8 %while.66 = (s32[]{:T(128)}, f32[128,384]{0,1:T(8,128)S(1)}, f32[49,6,128]{2,1,0:T(8,128)S(1)}, bf16[14,22,768]{2,1,0:T(8,128)(2,1)S(1)}, bf16[128,6,64]{2,1,0:T...) while((s32[]{:T(128)}, f32[128,384]{0,1:T(8,128)S(1)}, ...), condition=%wide.region_13.14_spmd, body=%wide.region_12.13_spmd.sunk | while | flops 394005 | bytes 2089296 | solution.py:229
  273.5 362.1 %while.67 = (s32[]{:T(128)}, f32[14,22,768]{2,1,0:T(8,128)}, f32[49,6,128]{1,2,0:T(8,128)}, bf16[14,22,768]{2,1,0:T(8,128)(2,1)S(1)}, bf16[128,6,64]{2,1,0:T(8,1...) while((s32[]{:T(128)}, f32[14,22,768]{2,1,0:T(8,128)}, ...), condition=%wide.region_15.16_spmd, body=%wide.region_14.15_spmd.sunk | while | flops 639765 | bytes 3960160 | solution.py:248
  277.5 3.5 dynamic_update_slice.25
  284.9 3.5 dynamic_update_slice.25
  292.3 3.5 dynamic_update_slice.25
  299.8 3.5 dynamic_update_slice.25
  307.2 3.5 dynamic_update_slice.25
  314.6 3.5 dynamic_update_slice.25
  322.1 3.5 dynamic_update_slice.25
  329.5 3.5 dynamic_update_slice.25
  336.9 3.5 dynamic_update_slice.25
  344.4 3.5 dynamic_update_slice.25
  351.8 3.5 dynamic_update_slice.25
  359.2 3.5 dynamic_update_slice.25
  366.7 3.5 dynamic_update_slice.25
  374.1 3.5 dynamic_update_slice.25
  381.5 3.5 dynamic_update_slice.25
  389.0 3.5 dynamic_update_slice.25
  396.4 3.5 dynamic_update_slice.25
  403.8 3.5 dynamic_update_slice.25
  411.3 3.5 dynamic_update_slice.25
  418.7 3.5 dynamic_update_slice.25
  426.1 3.5 dynamic_update_slice.25
  433.5 3.5 dynamic_update_slice.25
  441.0 3.5 dynamic_update_slice.25
  448.4 3.5 dynamic_update_slice.25
  455.8 3.5 dynamic_update_slice.25
  463.3 3.5 dynamic_update_slice.25
  470.7 3.5 dynamic_update_slice.25
  478.1 3.5 dynamic_update_slice.25
  485.6 3.4 dynamic_update_slice.25
  492.9 3.4 dynamic_update_slice.25
  647.5 3.4 collective-permute-start.5
  653.5 3.5 scatter-add.15
  657.9 3.8 collective-permute-start.6
  663.3 28.1 %all-reduce.2 = (bf16[16,384]{1,0:T(8,128)(2,1)S(1)}, bf16[16,384]{1,0:T(8,128)(2,1)S(1)}) all-reduce(bf16[16,384]{1,0:T(8,128)(2,1)S(1)} %convert_element_type.237, bf16[16,384]{1,0:T(8,128)(2,1)S(1)} %convert_element_type.229), channel_id=1, replica_groups=mesh['gy'=4,'gx'=8] {'gx'}, use_global_device_ids=true, to_apply=%region_18.19 | all-reduce | flops 12288 | bytes 49152 | tf_op jit(solution)/shard_map/psum | solution.py:203
  691.5 16.6 %all-reduce.3 = (bf16[8,384]{1,0:T(8,128)(2,1)S(1)}, bf16[8,384]{1,0:T(8,128)(2,1)S(1)}) all-reduce(bf16[8,384]{1,0:T(8,128)(2,1)S(1)} %convert_element_type.241, bf16[8,384]{1,0:T(8,128)(2,1)S(1)} %convert_element_type.233), channel_id=1, replica_groups=mesh['gy'=4,'gx'=8] {'gy'}, use_global_device_ids=true, to_apply=%region_19.20 | all-reduce | flops 6144 | bytes 24576 | tf_op jit(solution)/shard_map/psum | solution.py:207
  710.3 4.2 collective-permute-start.7
  (1505 shorter events, 440.8 us)
Async XLA Ops:
  0.6 1.2 copy-start
  0.6 71.7 %copy-start.2 = (bf16[384,384]{1,0:T(8,128)(2,1)S(1)}, bf16[384,384]{1,0:T(8,128)(2,1)}, u32[]{:S(2)}) copy-start(bf16[384,384]{1,0:T(8,128)(2,1)} %param.23) | copy-start | bytes 884740
  3.1 70.4 %collective-permute-start = (bf16[3,16,768]{2,1,0:T(8,128)(2,1)S(1)}, bf16[3,16,768]{2,1,0:T(8,128)(2,1)S(1)}, u32[]{:S(2)}, u32[]{:S(2)}) collective-permute-start(bf16[3,16,768]{2,1,0:T(8,128)(2,1)S(1)} %get-tuple-element.772), channel_id=1, source_target_pairs={{0,8},{8,16},{16,24},{1,9},{9,17},{17,25},{2,10},{10,18},{18,26},{... | collective-permute-start | bytes 221192 | tf_op jit(solution)/shard_map/ppermute | solution.py:20
  7.6 65.9 %collective-permute-start.1 = (bf16[3,16,768]{2,1,0:T(8,128)(2,1)S(1)}, bf16[3,16,768]{2,1,0:T(8,128)(2,1)S(1)}, u32[]{:S(2)}, u32[]{:S(2)}) collective-permute-start(bf16[3,16,768]{2,1,0:T(8,128)(2,1)S(1)} %get-tuple-element.773), channel_id=1, source_target_pairs={{8,0},{16,8},{24,16},{9,1},{17,9},{25,17},{10,2},{18,10},{26,18},{... | collective-permute-start | bytes 221192 | tf_op jit(solution)/shard_map/ppermute | solution.py:21
  41.0 67.2 %copy-start.1 = (bf16[128,384]{0,1:T(8,128)(2,1)}, bf16[128,384]{0,1:T(8,128)(2,1)S(1)}, u32[]{:S(2)}) copy-start(bf16[128,384]{0,1:T(8,128)(2,1)S(1)} %copy.82) | copy-start | bytes 294916
  73.6 35.1 %collective-permute-start.2 = (bf16[14,3,768]{2,1,0:T(4,128)(2,1)S(1)}, bf16[14,3,768]{2,1,0:T(4,128)(2,1)S(1)}, u32[]{:S(2)}, u32[]{:S(2)}) collective-permute-start(bf16[14,3,768]{2,1,0:T(4,128)(2,1)S(1)} %get-tuple-element.767), channel_id=1, source_target_pairs={{0,1},{1,2},{2,3},{3,4},{4,5},{5,6},{6,7},{8,9},{9,10},{10,11},{11... | collective-permute-start | bytes 193544 | tf_op jit(solution)/shard_map/ppermute | solution.py:20
  74.9 34.5 %collective-permute-start.3 = (bf16[14,3,768]{2,1,0:T(4,128)(2,1)S(1)}, bf16[14,3,768]{2,1,0:T(4,128)(2,1)}, u32[]{:S(2)}, u32[]{:S(2)}) collective-permute-start(bf16[14,3,768]{2,1,0:T(4,128)(2,1)S(1)} %get-tuple-element.768), channel_id=1, source_target_pairs={{1,0},{2,1},{3,2},{4,3},{5,4},{6,5},{7,6},{9,8},{10,9},{11,10},{12... | collective-permute-start | bytes 193544 | tf_op jit(solution)/shard_map/ppermute | solution.py:21
  108.7 0.6 copy-start.8
  147.7 79.6 %copy-start.3 = (f32[6,128]{1,0:T(8,128)}, f32[6,128]{1,0:T(8,128)S(1)}, u32[]{:S(2)}) copy-start(f32[6,128]{1,0:T(8,128)S(1)} %log_add_fusion) | copy-start | bytes 9220
  224.6 4.1 copy-start.4
  224.8 4.0 copy-start.5
  635.7 27.3 %copy-start.7 = (bf16[16,6,64]{2,0,1:T(8,128)(2,1)S(1)}, bf16[16,6,64]{2,0,1:T(8,128)(2,1)}, u32[]{:S(2)}) copy-start(bf16[16,6,64]{2,0,1:T(8,128)(2,1)} %fusion.18) | copy-start | bytes 36868
  636.7 5.8 collective-permute-start.4
  641.8 74.2 %copy-start.6 = (bf16[8,16,384]{2,1,0:T(8,128)(2,1)S(1)}, bf16[8,16,384]{2,1,0:T(8,128)(2,1)}, u32[]{:S(2)}) copy-start(bf16[8,16,384]{2,1,0:T(8,128)(2,1)} %param.25) | copy-start | bytes 294916
  647.5 5.0 collective-permute-start.5
  657.9 51.4 %collective-permute-start.6 = (bf16[3,16,768]{2,1,0:T(8,128)(2,1)S(1)}, bf16[3,16,768]{2,1,0:T(8,128)(2,1)S(1)}, u32[]{:S(2)}, u32[]{:S(2)}) collective-permute-start(bf16[3,16,768]{2,1,0:T(8,128)(2,1)S(1)} %slice.252), channel_id=1, source_target_pairs={{8,0},{16,8},{24,16},{9,1},{17,9},{25,17},{10,2},{18,10},{26,18},{... | collective-permute-start | bytes 221192 | tf_op jit(solution)/shard_map/ppermute | solution.py:29
  710.3 5.6 collective-permute-start.7
where the time goes:
time: 731 us; the launch traced here: 717 us
  local copies, waits for them, and re-layouts  356 us (49%)
  other arithmetic  177 us (24%)
  blocking collectives  133 us (18%)
  starting transfers between devices  21.7 us (3%)
  loops' own time  13.3 us (2%)
  matrix products  11.1 us (2%)
    dynamic_update_slice x49, local copies, waits for them, and re-layouts, return_step(): lax.dynamic_update_slice(ext_grad, updated, (position // KS, position % K...  169 us
    add x49, other arithmetic, return_step(): window(ext_grad, position) + jnp.concatenate([key_term, value_term], axis=2)  55.9 us
    transpose x49, other arithmetic, return_step(): score_grad.T[:, :, None] * query_heads * score_scale  42.1 us
    transpose x49, local copies, waits for them, and re-layouts, return_step(): probs.T[:, :, None] * datt_heads  41.7 us
    transpose x49, local copies, waits for them, and re-layouts, value_step(): return output + probs.T[:, :, None] * value_win  41.7 us
    psum x1, blocking collectives, local(): lax.psum(row_dv.astype(jnp.bfloat16), 'gx').astype(jnp.float32)  28.1 us
    unnamed x2, blocking collectives  25.5 us
    all_gather x1, blocking collectives, local(): lax.all_gather(pooled_keys, 'gx', axis=0, tiled=True)  21.7 us
  transfers between devices with their start and end apart: 8, of which 3 were waited for; matrix products, arithmetic and copies ran while one was open for 2% of the time, Pallas kernels for 0%

commit v1 on v0

--- a/solution.py
+++ b/solution.py
@@ -200,7 +200,7 @@
     block_count = pooled_keys.shape[0]
     whole_row_dk, whole_row_dv = (
         lax.psum(row_dk.astype(jnp.bfloat16), "gx").astype(jnp.float32),
-        lax.psum(row_dv.astype(jnp.bfloat16), "gx").astype(jnp.float32),
+        jnp.sum(lax.all_gather(row_dv.astype(jnp.bfloat16), "gx"), axis=0).astype(jnp.float32),
     )
     whole_col_dk, whole_col_dv = (
         lax.psum(col_dk.astype(jnp.bfloat16), "gy").astype(jnp.float32),

time: 731 us -> 797 us (1.090)
  local copies, waits for them, and re-layouts: 356 us -> 391 us
  blocking collectives: 133 us -> 163 us
    dynamic_slice x49, local copies, waits for them, and re-layouts: 4.44 us -> 37.7 us  [moving_window(): return lax.dynamic_slice(extended, starts, extent)]
    all_gather x0 -> x1, blocking collectives: none -> 24.5 us  [local(): lax.all_gather(row_dv.astype(jnp.bfloat16), 'gx')]
where the time goes in v1:
time: 797 us; the launch traced here: 782 us
  local copies, waits for them, and re-layouts  391 us (49%)
  other arithmetic  177 us (22%)
  blocking collectives  163 us (20%)
  starting transfers between devices  18.3 us (2%)
  loops' own time  12.8 us (2%)
  matrix products  12 us (2%)
    dynamic_update_slice x49, local copies, waits for them, and re-layouts, return_step(): lax.dynamic_update_slice(ext_grad, updated, (position // KS, position % K...  169 us
    add x49, other arithmetic, return_step(): window(ext_grad, position) + jnp.concatenate([key_term, value_term], axis=2)  55.9 us
    transpose x49, other arithmetic, return_step(): score_grad.T[:, :, None] * query_heads * score_scale  42.1 us
    transpose x49, local copies, waits for them, and re-layouts, return_step(): probs.T[:, :, None] * datt_heads  41.7 us
    transpose x49, local copies, waits for them, and re-layouts, value_step(): return output + probs.T[:, :, None] * value_win  41.7 us
    dynamic_slice x49, local copies, waits for them, and re-layouts, moving_window(): return lax.dynamic_slice(extended, starts, extent)  37.7 us
    psum x1, blocking collectives, local(): lax.psum(row_dk.astype(jnp.bfloat16), 'gx').astype(jnp.float32)  26.8 us
    unnamed x2, blocking collectives  25.5 us
  transfers between devices with their start and end apart: 8, of which 3 were waited for; matrix products, arithmetic and copies ran while one was open for 2% of the time, Pallas kernels for 0%

profile of v1, /device:TPU:1, one launch (start us, length us, event | category | flops | bytes accessed | tf_op | source)
XLA Modules:
  0.0 781.6 jit_solution(6960298157025809199)
XLA Ops:
  3.1 4.5 collective-permute-start
  9.6 21.7 %all-gather.2 = bf16[8,2,384]{2,1,0:T(2,128)(2,1)S(1)} all-gather(bf16[1,2,384]{2,1,0:T(2,128)(2,1)S(1)} %fusion.49), channel_id=1, replica_groups=mesh['gy'=4,'gx'=8] {'gx'}, dimensions={0}, use_global_device_ids=true | all-gather | bytes 13824 | tf_op jit(solution)/shard_map/all_gather | solution.py:89
  31.3 9.7 %all-gather.3 = bf16[4,2,384]{2,1,0:T(2,128)(2,1)S(1)} all-gather(bf16[1,2,384]{2,1,0:T(2,128)(2,1)S(1)} %fusion.49), channel_id=1, replica_groups=mesh['gy'=4,'gx'=8] {'gy'}, dimensions={0}, use_global_device_ids=true | all-gather | bytes 7680 | tf_op jit(solution)/shard_map/all_gather | solution.py:94
  44.1 16.2 %all-reduce = bf16[16]{0:T(256)(128)(2,1)S(1)} all-reduce(bf16[16]{0:T(256)(128)(2,1)S(1)} %dynamic-update-slice.12), channel_id=2, replica_groups=mesh['gy'=4,'gx'=8] {'gx'}, use_global_device_ids=true, to_apply=%add | all-reduce | flops 16 | bytes 64
  62.5 9.3 %all-reduce.1 = bf16[8]{0:T(256)(128)(2,1)S(1)} all-reduce(bf16[8]{0:T(256)(128)(2,1)S(1)} %dynamic-update-slice.13), channel_id=3, replica_groups=mesh['gy'=4,'gx'=8] {'gy'}, use_global_device_ids=true, to_apply=%add.1 | all-reduce | flops 8 | bytes 32
  78.7 21.3 %all-gather.4 = bf16[8,2,384]{2,1,0:T(2,128)(2,1)S(1)} all-gather(bf16[1,2,384]{2,1,0:T(2,128)(2,1)S(1)} %fusion.50), channel_id=1, replica_groups=mesh['gy'=4,'gx'=8] {'gx'}, dimensions={0}, use_global_device_ids=true | all-gather | bytes 13824 | tf_op jit(solution)/shard_map/all_gather | solution.py:90
  100.7 9.9 %all-gather.5 = bf16[4,2,384]{2,1,0:T(2,128)(2,1)S(1)} all-gather(bf16[1,2,384]{2,1,0:T(2,128)(2,1)S(1)} %fusion.50), channel_id=1, replica_groups=mesh['gy'=4,'gx'=8] {'gy'}, dimensions={0}, use_global_device_ids=true | all-gather | bytes 7680 | tf_op jit(solution)/shard_map/all_gather | solution.py:95
  112.2 69.8 %while.65 = (s32[]{:T(128)}, f32[49,6,128]{2,1,0:T(8,128)S(1)}, pred[14,22]{1,0:T(8,128)(4,1)}, bf16[14,22,768]{2,1,0:T(8,128)(2,1)S(1)}, bf16[128,6,64]{2,1,0:T...) while((s32[]{:T(128)}, f32[49,6,128]{2,1,0:T(8,128)S(1)}, ...), condition=%wide.region_1.0_spmd, body=%wide.region_0.0_spmd.sunk | while | flops 197396 | bytes 608564 | solution.py:110
  184.7 4.1 exp.21
  188.7 68.9 %while.68 = (s32[]{:T(128)}, f32[128,6,64]{2,1,0:T(8,128)S(1)}, f32[49,6,128]{1,2,0:T(8,128)}, bf16[14,22,768]{2,1,0:T(8,128)(2,1)S(1)}, s32[]{:T(128)}, /*index...) while((s32[]{:T(128)}, f32[128,6,64]{2,1,0:T(8,128)S(1)}, ...), condition=%wide.region_10.11_spmd.clone, body=%wide.region_9.10_spmd.clone.sunk | while | flops 196630 | bytes 1287498 | solution.py:146
  263.9 43.8 %while.66 = (s32[]{:T(128)}, f32[128,384]{0,1:T(8,128)S(1)}, f32[49,6,128]{2,1,0:T(8,128)S(1)}, bf16[14,22,768]{2,1,0:T(8,128)(2,1)S(1)}, bf16[128,6,64]{2,1,0:T...) while((s32[]{:T(128)}, f32[128,384]{0,1:T(8,128)S(1)}, ...), condition=%wide.region_13.14_spmd, body=%wide.region_12.13_spmd.sunk | while | flops 394005 | bytes 2089296 | solution.py:229
  308.8 362.1 %while.67 = (s32[]{:T(128)}, f32[14,22,768]{2,1,0:T(8,128)}, f32[49,6,128]{1,2,0:T(8,128)}, bf16[14,22,768]{2,1,0:T(8,128)(2,1)S(1)}, bf16[128,6,64]{2,1,0:T(8,1...) while((s32[]{:T(128)}, f32[14,22,768]{2,1,0:T(8,128)}, ...), condition=%wide.region_15.16_spmd, body=%wide.region_14.15_spmd.sunk | while | flops 639765 | bytes 3960160 | solution.py:248
  312.7 3.5 dynamic_update_slice.25
  320.2 3.5 dynamic_update_slice.25
  327.6 3.5 dynamic_update_slice.25
  335.0 3.5 dynamic_update_slice.25
  342.5 3.5 dynamic_update_slice.25
  349.9 3.5 dynamic_update_slice.25
  357.3 3.5 dynamic_update_slice.25
  364.8 3.5 dynamic_update_slice.25
  372.2 3.5 dynamic_update_slice.25
  379.6 3.5 dynamic_update_slice.25
  387.1 3.5 dynamic_update_slice.25
  394.5 3.5 dynamic_update_slice.25
  401.9 3.5 dynamic_update_slice.25
  409.4 3.5 dynamic_update_slice.25
  416.8 3.5 dynamic_update_slice.25
  424.2 3.5 dynamic_update_slice.25
  431.7 3.5 dynamic_update_slice.25
  439.1 3.5 dynamic_update_slice.25
  446.5 3.5 dynamic_update_slice.25
  453.9 3.5 dynamic_update_slice.25
  461.4 3.5 dynamic_update_slice.25
  468.8 3.5 dynamic_update_slice.25
  476.2 3.5 dynamic_update_slice.25
  483.7 3.5 dynamic_update_slice.25
  491.1 3.5 dynamic_update_slice.25
  498.5 3.5 dynamic_update_slice.25
  505.9 3.5 dynamic_update_slice.25
  513.4 3.5 dynamic_update_slice.25
  520.8 3.4 dynamic_update_slice.25
  528.2 3.4 dynamic_update_slice.25
  535.6 3.4 dynamic_update_slice.25
  682.7 3.5 collective-permute-start.5
  688.4 24.5 %all_gather.28 = bf16[8,16,384]{2,1,0:T(8,128)(2,1)S(1)} all-gather(bf16[1,16,384]{2,1,0:T(8,128)(2,1)S(1)} %convert_element_type.246), channel_id=1, replica_groups=mesh['gy'=4,'gx'=8] {'gx'}, dimensions={0}, use_global_device_ids=true | all-gather | bytes 110592 | tf_op jit(solution)/shard_map/all_gather | solution.py:203
  713.8 26.8 %psum.21 = bf16[16,384]{1,0:T(8,128)(2,1)S(1)} all-reduce(bf16[16,384]{1,0:T(8,128)(2,1)S(1)} %convert_element_type.238), channel_id=1, replica_groups=mesh['gy'=4,'gx'=8] {'gx'}, use_global_device_ids=true, to_apply=%region_16.17 | all-reduce | flops 6144 | bytes 24576 | tf_op jit(solution)/shard_map/psum | solution.py:202
  740.6 23.8 %all-reduce.2 = (bf16[8,384]{1,0:T(8,128)(2,1)S(1)}, bf16[8,384]{1,0:T(8,128)(2,1)S(1)}) all-reduce(bf16[8,384]{1,0:T(8,128)(2,1)S(1)} %convert_element_type.250, bf16[8,384]{1,0:T(8,128)(2,1)S(1)} %convert_element_type.242), channel_id=1, replica_groups=mesh['gy'=4,'gx'=8] {'gy'}, use_global_device_ids=true, to_apply=%region_19.20 | all-reduce | flops 6144 | bytes 24576 | tf_op jit(solution)/shard_map/psum | solution.py:207
  765.5 3.5 scatter-add.15
  (1516 shorter events, 479.9 us)
Async XLA Ops:
  0.6 1.2 copy-start
  0.6 72.9 %copy-start.2 = (bf16[384,384]{1,0:T(8,128)(2,1)S(1)}, bf16[384,384]{1,0:T(8,128)(2,1)}, u32[]{:S(2)}) copy-start(bf16[384,384]{1,0:T(8,128)(2,1)} %param.23) | copy-start | bytes 884740
  3.1 71.6 %collective-permute-start = (bf16[3,16,768]{2,1,0:T(8,128)(2,1)S(1)}, bf16[3,16,768]{2,1,0:T(8,128)(2,1)S(1)}, u32[]{:S(2)}, u32[]{:S(2)}) collective-permute-start(bf16[3,16,768]{2,1,0:T(8,128)(2,1)S(1)} %get-tuple-element.770), channel_id=1, source_target_pairs={{0,8},{8,16},{16,24},{1,9},{9,17},{17,25},{2,10},{10,18},{18,26},{... | collective-permute-start | bytes 221192 | tf_op jit(solution)/shard_map/ppermute | solution.py:20
  7.6 67.1 %collective-permute-start.1 = (bf16[3,16,768]{2,1,0:T(8,128)(2,1)S(1)}, bf16[3,16,768]{2,1,0:T(8,128)(2,1)S(1)}, u32[]{:S(2)}, u32[]{:S(2)}) collective-permute-start(bf16[3,16,768]{2,1,0:T(8,128)(2,1)S(1)} %get-tuple-element.771), channel_id=1, source_target_pairs={{8,0},{16,8},{24,16},{9,1},{17,9},{25,17},{10,2},{18,10},{26,18},{... | collective-permute-start | bytes 221192 | tf_op jit(solution)/shard_map/ppermute | solution.py:21
  41.0 221.8 %copy-start.1 = (bf16[128,384]{0,1:T(8,128)(2,1)}, bf16[128,384]{0,1:T(8,128)(2,1)S(1)}, u32[]{:S(2)}) copy-start(bf16[128,384]{0,1:T(8,128)(2,1)S(1)} %copy.82) | copy-start | bytes 294916
  44.1 34.2 %copy-start.5 = (bf16[16,6,64]{2,1,0:T(8,128)(2,1)}, bf16[16,6,64]{2,1,0:T(8,128)(2,1)S(1)}, u32[]{:S(2)}) copy-start(bf16[16,6,64]{2,1,0:T(8,128)(2,1)S(1)} %reshape.422) | copy-start | bytes 36868
  62.5 11.0 %copy-start.8 = (bf16[8,6,64]{2,1,0:T(8,128)(2,1)}, bf16[8,6,64]{2,1,0:T(8,128)(2,1)S(1)}, u32[]{:S(2)}) copy-start(bf16[8,6,64]{2,1,0:T(8,128)(2,1)S(1)} %reshape.423) | copy-start | bytes 18436
  74.8 36.3 %collective-permute-start.2 = (bf16[14,3,768]{2,1,0:T(4,128)(2,1)S(1)}, bf16[14,3,768]{2,1,0:T(4,128)(2,1)S(1)}, u32[]{:S(2)}, u32[]{:S(2)}) collective-permute-start(bf16[14,3,768]{2,1,0:T(4,128)(2,1)S(1)} %get-tuple-element.765), channel_id=1, source_target_pairs={{0,1},{1,2},{2,3},{3,4},{4,5},{5,6},{6,7},{8,9},{9,10},{10,11},{11... | collective-permute-start | bytes 193544 | tf_op jit(solution)/shard_map/ppermute | solution.py:20
  76.1 35.0 %collective-permute-start.3 = (bf16[14,3,768]{2,1,0:T(4,128)(2,1)S(1)}, bf16[14,3,768]{2,1,0:T(4,128)(2,1)}, u32[]{:S(2)}, u32[]{:S(2)}) collective-permute-start(bf16[14,3,768]{2,1,0:T(4,128)(2,1)S(1)} %get-tuple-element.766), channel_id=1, source_target_pairs={{1,0},{2,1},{3,2},{4,3},{5,4},{6,5},{7,6},{9,8},{10,9},{11,10},{12... | collective-permute-start | bytes 193544 | tf_op jit(solution)/shard_map/ppermute | solution.py:21
  112.2 69.8 %copy-start.11 = (f32[6,128]{1,0:T(8,128)S(1)}, f32[6,128]{1,0:T(8,128)}, u32[]{:S(2)}) copy-start(f32[6,128]{1,0:T(8,128)} %get-tuple-element.776) | copy-start | bytes 9220
  112.2 69.8 %copy-start.12 = (f32[6,128]{1,0:T(8,128)S(1)}, f32[6,128]{1,0:T(8,128)}, u32[]{:S(2)}) copy-start(f32[6,128]{1,0:T(8,128)} %get-tuple-element.774) | copy-start | bytes 9220
  182.2 79.6 %copy-start.3 = (f32[6,128]{1,0:T(8,128)}, f32[6,128]{1,0:T(8,128)S(1)}, u32[]{:S(2)}) copy-start(f32[6,128]{1,0:T(8,128)S(1)} %log_add_fusion) | copy-start | bytes 9220
  188.7 69.1 %copy-start.4 = (bf16[16,6,64]{2,1,0:T(8,128)(2,1)S(1)}, bf16[16,6,64]{2,1,0:T(8,128)(2,1)}, u32[]{:S(2)}) copy-start(bf16[16,6,64]{2,1,0:T(8,128)(2,1)} %reshape.424) | copy-start | bytes 36868
  257.6 5.0 copy-start.6
  257.6 6.1 copy-start.9
  259.2 4.7 copy-start.7
  671.9 5.8 collective-permute-start.4
  676.8 103.7 %copy-start.10 = (bf16[8,16,384]{2,1,0:T(8,128)(2,1)S(1)}, bf16[8,16,384]{2,1,0:T(8,128)(2,1)}, u32[]{:S(2)}) copy-start(bf16[8,16,384]{2,1,0:T(8,128)(2,1)} %param.25) | copy-start | bytes 294916
  682.7 81.7 %collective-permute-start.5 = (bf16[14,3,768]{2,1,0:T(4,128)(2,1)S(1)}, bf16[14,3,768]{2,1,0:T(4,128)(2,1)S(1)}, u32[]{:S(2)}, u32[]{:S(2)}) collective-permute-start(bf16[14,3,768]{2,1,0:T(4,128)(2,1)S(1)} %slice.249), channel_id=1, source_target_pairs={{0,1},{1,2},{2,3},{3,4},{4,5},{5,6},{6,7},{8,9},{9,10},{10,11},{11... | collective-permute-start | bytes 193544 | tf_op jit(solution)/shard_map/ppermute | solution.py:29
  769.9 6.2 collective-permute-start.6
  777.1 3.3 collective-permute-start.7
